TPU v7x, 32 devices: a whole 2x2x4 slice. The times are simulated.
32 devices in a mesh: dp: 2 (over core), seq: 16 (over z, y, x).
Axes of the slice: x: 2, y: 2, z: 4, core: 2. Of those that a mesh axis runs over, the one named last changes fastest.
Arguments:
- tokens: bfloat16 [32768, 768], P(('dp', 'seq')), may hold values from -6 to 6
- doc_start: int32 [32768], P(('dp', 'seq')), may hold values from 0 to 32767, as said below
- real: int32 [32768], P(('dp', 'seq')), may hold values from 0 to 1, as said below
- w_qkv: bfloat16 [768, 2304], P('dp', 'seq'), may hold values from -0.3125 to 0.3125
- w_out: bfloat16 [768, 768], P('dp', 'seq'), may hold values from -1 to 1
- w_in: bfloat16 [768, 2304], P('dp', 'seq'), may hold values from -0.21875 to 0.21875
- w_down: bfloat16 [1152, 768], P('dp', 'seq'), may hold values from -0.375 to 0.375
- gain_attn: bfloat16 [768], P('seq'), may hold values from 0.5 to 1.5
- gain_mlp: bfloat16 [768], P('seq'), may hold values from 0.5 to 1.5
- cotangent: bfloat16 [32768, 768], P(('dp', 'seq')), may hold values from -6 to 6
Outputs:
- output: bfloat16 [32768, 768], P(('dp', 'seq'))
- grad_tokens: float32 [32768, 768], P(('dp', 'seq'))
- grad_w_qkv: float32 [768, 2304], P('dp', 'seq')
- grad_w_out: float32 [768, 768], P('dp', 'seq')
- grad_w_in: float32 [768, 2304], P('dp', 'seq')
- grad_w_down: float32 [1152, 768], P('dp', 'seq')
- grad_gain_attn: float32 [768], P('seq')
- grad_gain_mlp: float32 [768], P('seq')
Inputs may be any that keep to these rules, and one draw needn't show every extreme that they name: `doc_start`: for each slot, the index in the whole stream of 32768 slots of the first slot of its document; packed rows begin at slots 8192 / 2 + k * 8192, so the first and the last row hold 4096 slots and the others 8192; documents never cross a row, and a row's padding forms a document of its own. `real`: each packed row ends in one or more padding slots and has no others.
All inputs are finite; a program needn't handle non-finite values.
Results may differ from a plain program's by a relative error of at most 0.014.
The roundings to bfloat16 on the way count: a program that leaves them out, or rounds other values in their place, can miss the bound.
Values may be sent and summed in bfloat16 or wider, within the bound.
A program may use at most 192 MiB of HBM per device.

v0:
```python
import functools
import math

import jax
import jax.numpy as jnp
from jax import lax
from jax.experimental import pallas as pl
from jax.experimental.pallas import tpu as pltpu
from jax.sharding import PartitionSpec as P

D = 768
HEADS = 12
HEAD = 64
FF = 1152
HALF = 64


def padded(value, sides, width):
    for axis, dim in sides:
        size, length = (lax.axis_size(axis), value.shape[dim])
        up = [(i, (i + 1) % size) for i in range(size - 1)]
        down = [(j, i) for i, j in up]
        last = lax.slice_in_dim(value, length - width, length, axis=dim)
        initial = lax.slice_in_dim(value, 0, width, axis=dim)
        before = lax.ppermute(last, axis, up)
        after = lax.ppermute(initial, axis, down)
        value = jnp.concatenate([before, value, after], axis=dim)
    return value


def shifted(value, axis, by):
    length = lax.axis_size(axis)
    pairs = [(i, i + by) for i in range(length) if 0 <= i + by < length]
    return lax.ppermute(value, axis, pairs)


def layer_norm(value):
    centre = value - jnp.mean(value, axis=-1, keepdims=True)
    factor = lax.rsqrt(jnp.mean(centre * centre, axis=-1, keepdims=True) + 1e-05)
    return (centre * factor, factor)


def norm_back(grad, normed, factor):
    return factor * (
        grad
        - jnp.mean(grad, axis=-1, keepdims=True)
        - normed * jnp.mean(grad * normed, axis=-1, keepdims=True)
    )


def rotary_tables(place):
    freq = jnp.exp(jnp.arange(HEAD // 2, dtype=jnp.float32) * (-2.0 * math.log(10000.0) / HEAD))
    angle = place[:, None] * freq[None, :]
    cosine = jnp.tile(jnp.concatenate([jnp.cos(angle), jnp.cos(angle)], 1), (1, HEADS))
    sine = jnp.tile(jnp.concatenate([jnp.sin(angle), jnp.sin(angle)], 1), (1, HEADS))
    return (cosine, sine)


def rotate(value):
    count = value.shape[0]
    shaped = value.reshape(count, HEADS, HEAD)
    first = shaped[..., : HEAD // 2]
    second = shaped[..., HEAD // 2 :]
    return jnp.concatenate([-second, first], -1).reshape(count, HEADS * HEAD)


def left_dot(left, right):
    return lax.dot_general(
        left, right, (((0,), (0,)), ((), ())), preferred_element_type=jnp.float32
    )


def right_dot(left, right):
    return lax.dot_general(
        left, right, (((1,), (1,)), ((), ())), preferred_element_type=jnp.float32
    )


def glu_piece(gate_up):
    return jax.nn.gelu(gate_up[:, :FF], approximate=False) * gate_up[:, FF:]


MESH = pl.DeviceIdType.MESH


def ring_order(mesh):
    n = mesh.shape["seq"]
    try:
        coords = [tuple(mesh.devices[0, s].coords) for s in range(n)]
    except Exception:
        return list(range(n))
    near = [
        [t for t in range(n) if sum(abs(a - b) for a, b in zip(coords[s], coords[t])) == 1]
        for s in range(n)
    ]
    path, seen = [0], {0}

    def grow(budget=[200000]):
        budget[0] -= 1
        if budget[0] < 0:
            return False
        if len(path) == n:
            return 0 in near[path[-1]]
        options = sorted(
            (t for t in near[path[-1]] if t not in seen),
            key=lambda t: sum(1 for u in near[t] if u not in seen),
        )
        for t in options:
            path.append(t)
            seen.add(t)
            if grow():
                return True
            path.pop()
            seen.discard(t)
        return False

    return list(path) if n > 2 and grow() else list(range(n))


def lookup(index, table):
    n = len(table)
    square = n * n
    total = jnp.int32(0)
    for k, value in enumerate(table):
        if value:
            gap = index - k
            differs = lax.div(gap * gap + (square - 1), jnp.int32(square))
            total = total + value * (1 - differs)
    return total


def ring_kernel(order, per_way, h_ref, out_ref, recv, send, ssem, rsem, free):
    n = len(order)
    where = [0] * n
    for p, s in enumerate(order):
        where[s] = p
    d = lax.axis_index("dp")
    me = lax.axis_index("seq")
    pos = lookup(me, where)
    nxt = lookup(lax.rem(pos + 1, n), order)
    prv = lookup(lax.rem(pos + n - 1, n), order)
    piece = out_ref.shape[0] // per_way
    ahead = (n - 1) // 2
    behind = n - 1 - ahead

    barrier = pltpu.get_barrier_semaphore()
    pl.semaphore_signal(barrier, 1, device_id=(d, nxt), device_id_type=MESH)
    pl.semaphore_signal(barrier, 1, device_id=(d, prv), device_id_type=MESH)
    pl.semaphore_wait(barrier, 2)

    lanes = []
    for forward in (True, False):
        for chunk in range(per_way):
            li = len(lanes)
            lanes.append((recv.at[li], send.at[li], ssem.at[li], rsem.at[li], free.at[li],
                          nxt if forward else prv, prv if forward else nxt,
                          slice(chunk * piece, (chunk + 1) * piece),
                          ahead if forward else behind, forward))
    copies = {}
    for step in range(max(ahead, behind)):
        slot = step % 2
        for li, (recv, send, ssem, rsem, free, to, frm, rows, sends, forward) in enumerate(lanes):
            if step >= sends:
                continue
            if forward:
                target = pos + sends - step
            else:
                target = pos + n - sends + step
            q = lookup(lax.rem(target, n), order)
            own = h_ref[q, rows, :].astype(jnp.float32)
            if step == 0:
                part = own
            else:
                copies[(li, step - 1)].wait_recv()
                part = recv[1 - slot].astype(jnp.float32) + own
                if step <= sends - 2:
                    pl.semaphore_signal(free, 1, device_id=(d, frm), device_id_type=MESH)
            if step >= 2:
                copies[(li, step - 2)].wait_send()
                pl.semaphore_wait(free, 1)
            send[slot] = part.astype(send.dtype)
            c = pltpu.make_async_remote_copy(
                src_ref=send.at[slot], dst_ref=recv.at[slot],
                send_sem=ssem.at[slot], recv_sem=rsem.at[slot],
                device_id=(d, to), device_id_type=MESH)
            c.start()
            copies[(li, step)] = c
    for chunk in range(per_way):
        rows = lanes[chunk][7]
        total = h_ref[me, rows, :].astype(jnp.float32)
        for li in (chunk, per_way + chunk):
            recv, sends = lanes[li][0], lanes[li][8]
            copies[(li, sends - 1)].wait_recv()
            total = total + recv[(sends - 1) % 2].astype(jnp.float32)
        out_ref[rows, :] = total
    for li, lane in enumerate(lanes):
        sends = lane[8]
        if sends >= 2:
            copies[(li, sends - 2)].wait_send()
        copies[(li, sends - 1)].wait_send()


RING_WAYS = 2


def ring_reduce(h, order, per_way, link_dtype=jnp.bfloat16):
    n, rows, width = h.shape
    lanes = 2 * per_way
    piece = rows // per_way
    return pl.pallas_call(
        functools.partial(ring_kernel, tuple(order), per_way),
        out_shape=jax.ShapeDtypeStruct((rows, width), jnp.float32),
        in_specs=[pl.BlockSpec(memory_space=pltpu.VMEM)],
        out_specs=pl.BlockSpec(memory_space=pltpu.VMEM),
        scratch_shapes=[
            pltpu.VMEM((lanes, 2, piece, width), link_dtype),
            pltpu.VMEM((lanes, 2, piece, width), link_dtype),
            pltpu.SemaphoreType.DMA((lanes, 2)),
            pltpu.SemaphoreType.DMA((lanes, 2)),
            pltpu.SemaphoreType.REGULAR((lanes,)),
        ],
        compiler_params=pltpu.CompilerParams(collective_id=1, has_side_effects=True,
                                             vmem_limit_bytes=48 * 1024 * 1024),
    )(h)


QB = 256


def window_allow(tq_ref, tk_ref, a0, w0):
    rows = lax.broadcasted_iota(jnp.int32, (QB, QB + 2 * HALF), 0)
    cols = lax.broadcasted_iota(jnp.int32, (QB, QB + 2 * HALF), 1)
    offset = cols - rows - HALF
    near = jnp.abs(offset) <= HALF
    same = tk_ref[:, pl.ds(w0, QB + 2 * HALF)] == tq_ref[pl.ds(a0, QB), :]
    return near & (same | (offset == 0))


def nt(a, b):
    return lax.dot_general(a, b, (((1,), (1,)), ((), ())), preferred_element_type=jnp.float32)


def tn(a, b):
    return lax.dot_general(a, b, (((0,), (0,)), ((), ())), preferred_element_type=jnp.float32)


def probs_of(q_ref, kv_ref, allow, a0, w0, h):
    q_h = q_ref[pl.ds(a0, QB), pl.ds(h * HEAD, HEAD)]
    k_h = kv_ref[pl.ds(w0, QB + 2 * HALF), pl.ds(h * HEAD, HEAD)]
    scores = jnp.where(allow, nt(q_h, k_h) * 0.125, -1e30)
    largest = jnp.max(scores, axis=-1, keepdims=True)
    raised = jnp.exp(scores - largest)
    return raised / jnp.sum(raised, axis=-1, keepdims=True), q_h, k_h


def neighbours():
    n_seq = lax.axis_size("seq")
    total = lax.axis_size("dp") * n_seq
    me = lax.axis_index("dp") * n_seq + lax.axis_index("seq")
    before = lax.rem(me + total - 1, total)
    after = lax.rem(me + 1, total)
    return (
        (lax.div(before, n_seq), lax.rem(before, n_seq)),
        (lax.div(after, n_seq), lax.rem(after, n_seq)),
    )


def greet(before, after):
    barrier = pltpu.get_barrier_semaphore()
    pl.semaphore_signal(barrier, 1, device_id=before, device_id_type=MESH)
    pl.semaphore_signal(barrier, 1, device_id=after, device_id_type=MESH)
    return barrier


def start_of(b):
    return b * QB if isinstance(b, int) else pl.multiple_of(b * QB, QB)


def attn_fwd_kernel(q_ref, kv_ref, tq_ref, tk_ref, o_ref, lo_ref, hi_ref, wide, send_sem, recv_sem):
    width = q_ref.shape[1]
    count = q_ref.shape[0]
    blocks = count // QB
    before, after = neighbours()
    barrier = greet(before, after)
    to_before = pltpu.make_async_remote_copy(
        src_ref=kv_ref.at[pl.ds(0, HALF)], dst_ref=hi_ref,
        send_sem=send_sem.at[0], recv_sem=recv_sem.at[0],
        device_id=before, device_id_type=MESH)
    to_after = pltpu.make_async_remote_copy(
        src_ref=kv_ref.at[pl.ds(count - HALF, HALF)], dst_ref=lo_ref,
        send_sem=send_sem.at[1], recv_sem=recv_sem.at[1],
        device_id=after, device_id_type=MESH)
    wide[pl.ds(HALF, count), :] = kv_ref[...]

    def block(b, carry):
        a0 = start_of(b)
        allow = window_allow(tq_ref, tk_ref, a0, a0)
        for h in range(HEADS):
            probs, _, _ = probs_of(q_ref, wide, allow, a0, a0, h)
            v_h = wide[pl.ds(a0, QB + 2 * HALF), pl.ds(width + h * HEAD, HEAD)]
            mixed = jnp.dot(probs.astype(jnp.bfloat16), v_h, preferred_element_type=jnp.float32)
            o_ref[pl.ds(a0, QB), pl.ds(h * HEAD, HEAD)] = mixed.astype(o_ref.dtype)
        return carry

    block(1, 0)
    pl.semaphore_wait(barrier, 2)
    to_before.start()
    to_after.start()
    lax.fori_loop(2, blocks - 1, block, 0)
    to_before.wait_recv()
    to_after.wait_recv()
    wide[pl.ds(0, HALF), :] = lo_ref[...]
    wide[pl.ds(count + HALF, HALF), :] = hi_ref[...]
    block(0, 0)
    block(blocks - 1, 0)
    to_before.wait_send()
    to_after.wait_send()


def attn_bwd_kernel(q_ref, kv_ref, lo_ref, hi_ref, tq_ref, tk_ref, do_ref, dq_ref, dkv_ref,
                    wide, dwide, send_lo, send_hi, recv_lo, recv_hi, send_sem, recv_sem):
    width = q_ref.shape[1]
    count = q_ref.shape[0]
    blocks = count // QB
    before, after = neighbours()
    barrier = greet(before, after)
    wide[pl.ds(0, HALF), :] = lo_ref[...]
    wide[pl.ds(HALF, count), :] = kv_ref[...]
    wide[pl.ds(count + HALF, HALF), :] = hi_ref[...]
    dwide[...] = jnp.zeros(dwide.shape, dwide.dtype)

    def block(b, carry):
        a0 = start_of(b)
        allow = window_allow(tq_ref, tk_ref, a0, a0)
        for h in range(HEADS):
            probs, q_h, k_h = probs_of(q_ref, wide, allow, a0, a0, h)
            v_h = wide[pl.ds(a0, QB + 2 * HALF), pl.ds(width + h * HEAD, HEAD)]
            do_h = do_ref[pl.ds(a0, QB), pl.ds(h * HEAD, HEAD)]
            grad_probs = nt(do_h, v_h)
            inner = jnp.sum(probs * grad_probs, axis=-1, keepdims=True)
            grad_scores = (probs * (grad_probs - inner)).astype(jnp.bfloat16)
            dq_ref[pl.ds(a0, QB), pl.ds(h * HEAD, HEAD)] = (
                jnp.dot(grad_scores, k_h, preferred_element_type=jnp.float32) * 0.125
            )
            rows = pl.ds(a0, QB + 2 * HALF)
            dwide[rows, pl.ds(h * HEAD, HEAD)] += tn(grad_scores, q_h) * 0.125
            dwide[rows, pl.ds(width + h * HEAD, HEAD)] += tn(probs.astype(jnp.bfloat16), do_h)
        return carry

    block(0, 0)
    block(blocks - 1, 0)
    send_lo[...] = dwide[pl.ds(0, HALF), :].astype(send_lo.dtype)
    send_hi[...] = dwide[pl.ds(count + HALF, HALF), :].astype(send_hi.dtype)
    to_before = pltpu.make_async_remote_copy(
        src_ref=send_lo, dst_ref=recv_hi,
        send_sem=send_sem.at[0], recv_sem=recv_sem.at[0],
        device_id=before, device_id_type=MESH)
    to_after = pltpu.make_async_remote_copy(
        src_ref=send_hi, dst_ref=recv_lo,
        send_sem=send_sem.at[1], recv_sem=recv_sem.at[1],
        device_id=after, device_id_type=MESH)
    pl.semaphore_wait(barrier, 2)
    to_before.start()
    to_after.start()
    lax.fori_loop(1, blocks - 1, block, 0)
    dkv_ref[...] = dwide[pl.ds(HALF, count), :]
    to_before.wait_recv()
    to_after.wait_recv()
    dkv_ref[pl.ds(0, HALF), :] += recv_lo[...].astype(jnp.float32)
    dkv_ref[pl.ds(count - HALF, HALF), :] += recv_hi[...].astype(jnp.float32)
    to_before.wait_send()
    to_after.wait_send()


VMEM_LIMIT = 48 * 1024 * 1024


def attn_fwd(query, kv, tag_q, tag_k):
    count, width = query.shape
    vm = pl.BlockSpec(memory_space=pltpu.VMEM)
    halo = jax.ShapeDtypeStruct((HALF, kv.shape[1]), kv.dtype)
    return pl.pallas_call(
        attn_fwd_kernel,
        out_shape=(jax.ShapeDtypeStruct((count, width), jnp.bfloat16), halo, halo),
        in_specs=[vm] * 4,
        out_specs=(vm, vm, vm),
        scratch_shapes=[
            pltpu.VMEM((count + 2 * HALF, kv.shape[1]), kv.dtype),
            pltpu.SemaphoreType.DMA((2,)),
            pltpu.SemaphoreType.DMA((2,)),
        ],
        compiler_params=pltpu.CompilerParams(
            collective_id=2, has_side_effects=True, vmem_limit_bytes=VMEM_LIMIT
        ),
    )(query, kv, tag_q.reshape(count, 1), tag_k.reshape(1, -1))


def attn_bwd(query, kv, lo, hi, tag_q, tag_k, grad_out):
    count, width = query.shape
    vm = pl.BlockSpec(memory_space=pltpu.VMEM)
    return pl.pallas_call(
        attn_bwd_kernel,
        out_shape=(
            jax.ShapeDtypeStruct((count, width), jnp.float32),
            jax.ShapeDtypeStruct(kv.shape, jnp.float32),
        ),
        in_specs=[vm] * 7,
        out_specs=(vm, vm),
        scratch_shapes=[
            pltpu.VMEM((count + 2 * HALF, kv.shape[1]), kv.dtype),
            pltpu.VMEM((count + 2 * HALF, kv.shape[1]), jnp.float32),
            pltpu.VMEM((HALF, kv.shape[1]), jnp.bfloat16),
            pltpu.VMEM((HALF, kv.shape[1]), jnp.bfloat16),
            pltpu.VMEM((HALF, kv.shape[1]), jnp.bfloat16),
            pltpu.VMEM((HALF, kv.shape[1]), jnp.bfloat16),
            pltpu.SemaphoreType.DMA((2,)),
            pltpu.SemaphoreType.DMA((2,)),
        ],
        compiler_params=pltpu.CompilerParams(
            collective_id=3, has_side_effects=True, vmem_limit_bytes=VMEM_LIMIT
        ),
    )(query, kv, lo, hi, tag_q.reshape(count, 1), tag_k.reshape(1, -1), grad_out)


ROPE_ROWS = 256


def head_rotate(x):
    width = x.shape[-1]
    lane = lax.broadcasted_iota(jnp.int32, x.shape, x.ndim - 1)
    ahead = pltpu.roll(x, width - HEAD // 2, x.ndim - 1)
    behind = pltpu.roll(x, HEAD // 2, x.ndim - 1)
    return jnp.where(lane % HEAD < HEAD // 2, -ahead, behind)


def rope_fwd_kernel(qkv_ref, cos_ref, sin_ref, q_ref, kv_ref):
    width = q_ref.shape[1]
    c = cos_ref[...]
    s = sin_ref[...]
    q = qkv_ref[:, pl.ds(0, width)]
    k = qkv_ref[:, pl.ds(width, width)]
    q_ref[...] = (q * c + head_rotate(q) * s).astype(q_ref.dtype)
    kv_ref[:, pl.ds(0, width)] = (k * c + head_rotate(k) * s).astype(kv_ref.dtype)
    kv_ref[:, pl.ds(width, width)] = qkv_ref[:, pl.ds(2 * width, width)].astype(kv_ref.dtype)


def rope_bwd_kernel(dq_ref, dkv_ref, cos_ref, sin_ref, out_ref):
    width = dq_ref.shape[1]
    c = cos_ref[...]
    s = sin_ref[...]
    dq = dq_ref[...]
    dk = dkv_ref[:, pl.ds(0, width)]
    out_ref[:, pl.ds(0, width)] = (dq * c - head_rotate(dq) * s).astype(out_ref.dtype)
    out_ref[:, pl.ds(width, width)] = (dk * c - head_rotate(dk) * s).astype(out_ref.dtype)
    out_ref[:, pl.ds(2 * width, width)] = dkv_ref[:, pl.ds(width, width)].astype(out_ref.dtype)


def rows_spec(cols):
    return pl.BlockSpec((ROPE_ROWS, cols), lambda i: (i, 0))


def rope_fwd(qkv, cosine, sine):
    count, width = cosine.shape
    return pl.pallas_call(
        rope_fwd_kernel,
        grid=(count // ROPE_ROWS,),
        out_shape=(
            jax.ShapeDtypeStruct((count, width), jnp.bfloat16),
            jax.ShapeDtypeStruct((count, 2 * width), jnp.bfloat16),
        ),
        in_specs=[rows_spec(3 * width), rows_spec(width), rows_spec(width)],
        out_specs=(rows_spec(width), rows_spec(2 * width)),
    )(qkv, cosine, sine)


def rope_bwd(dq, dkv, cosine, sine):
    count, width = cosine.shape
    return pl.pallas_call(
        rope_bwd_kernel,
        grid=(count // ROPE_ROWS,),
        out_shape=jax.ShapeDtypeStruct((count, 3 * width), jnp.bfloat16),
        in_specs=[rows_spec(width), rows_spec(2 * width), rows_spec(width), rows_spec(width)],
        out_specs=rows_spec(3 * width),
    )(dq, dkv, cosine, sine)


def down_lines_of(block, width):
    cols, extra = block.shape[0] // 2, block.shape[1] - width
    return block[:, :width], jnp.concatenate([block[:cols, width:], block[cols:, width:]], 1)


def down_from_lines(lines, width):
    cols = lines.shape[2] * 2 // 3
    extra = width // 2
    head, tail = lines[:, :, :cols], lines[:, :, cols:]
    tail = jnp.concatenate([tail[..., :extra], tail[..., extra:]], 2)
    return jnp.concatenate([head, tail], 3)


def gain_rows(gain, width, rows=8):
    line = jnp.pad(gain, (0, width - gain.shape[0]))
    return jnp.concatenate([line[None], jnp.zeros((rows - 1, width), gain.dtype)], 0)


def gather_rows(payload, n_dp, n_seq):
    every = lax.all_gather(payload, ("dp", "seq"), axis=0, tiled=True)
    return every.reshape(n_dp, n_seq, payload.shape[0], payload.shape[1])


def gain_blocks(grad_gain, n_dp, n_seq, width, height=8):
    part = jnp.pad(grad_gain.reshape(n_seq, -1), ((0, 0), (0, width - grad_gain.shape[0] // n_seq)))
    rows = jnp.concatenate([part[:, None], jnp.zeros((n_seq, height - 1, width), part.dtype)], 1)
    return jnp.broadcast_to(rows[None], (n_dp, n_seq, height, width))


def front(value, n_dp):
    return value.reshape(value.shape[0], n_dp, -1)


def apply_t(left, weight_t, n_dp):
    return jnp.einsum("tdr,dnr->tn", front(left, n_dp), weight_t, preferred_element_type=jnp.float32)


def apply_back(grad, weight_t):
    out = jnp.einsum("tn,dnr->tdr", grad, weight_t, preferred_element_type=jnp.float32)
    return out.reshape(out.shape[0], -1)


def grad_t(grad, left, n_dp):
    width = left.shape[1] // n_dp
    return [
        lax.dot_general(
            grad,
            left[:, d * width : (d + 1) * width],
            (((0,), (0,)), ((), ())),
            preferred_element_type=jnp.float32,
        )
        for d in range(n_dp)
    ]


def on_device(order, tokens, doc_start, real, w_qkv, w_out, w_in, w_down, gain_attn, gain_mlp, cotangent):
    count = tokens.shape[0]
    n_dp, n_seq = lax.axis_size("dp"), lax.axis_size("seq")
    rows, qkv_cols = w_qkv.shape
    out_cols, in_cols = w_out.shape[1], w_in.shape[1]
    down_rows, down_cols = w_down.shape
    down_lines = down_rows * down_cols // rows
    first = gather_rows(
        jnp.concatenate([w_qkv.T, w_out.T, gain_rows(gain_attn, rows)], 0), n_dp, n_seq
    )
    second = gather_rows(
        jnp.concatenate([w_in.T, *down_lines_of(w_down.T, rows), gain_rows(gain_mlp, rows)], 0),
        n_dp,
        n_seq,
    )
    full_qkv = first[:, :, :qkv_cols].reshape(n_dp, n_seq * qkv_cols, rows)
    full_out = first[:, :, qkv_cols : qkv_cols + out_cols].reshape(n_dp, n_seq * out_cols, rows)
    gain_one = (
        first[0, :, qkv_cols + out_cols, : gain_attn.shape[0]].reshape(-1).astype(jnp.float32)
    )
    stream = tokens.astype(jnp.float32)
    normed_a, factor_a = layer_norm(stream)
    h_attn = (normed_a * gain_one).astype(jnp.bfloat16)
    qkv = apply_t(h_attn, full_qkv, n_dp)
    offset_base = lax.axis_index(("dp", "seq")) * count
    place = (offset_base + jnp.arange(count, dtype=jnp.int32) - doc_start).astype(jnp.float32)
    cosine, sine = rotary_tables(place)
    query, key_value = rope_fwd(qkv, cosine, sine)
    tag_query = doc_start + 1
    tag_key = jnp.where(real == 1, tag_query, 0)
    wide_tag = padded(tag_key, ((("dp", "seq"), 0),), HALF)
    attn_out, halo_lo, halo_hi = attn_fwd(query, key_value, tag_query, wide_tag)
    mid = stream + apply_t(attn_out, full_out, n_dp)
    mid, second = lax.optimization_barrier((mid, second))
    at = 0
    full_in = second[:, :, at : at + in_cols].reshape(n_dp, n_seq * in_cols, rows)
    at += in_cols
    full_down = down_from_lines(second[:, :, at : at + down_lines], rows).reshape(
        n_dp, n_seq * down_cols, down_rows
    )
    at += down_lines
    gain_two = second[0, :, at, : gain_mlp.shape[0]].reshape(-1).astype(jnp.float32)
    normed_m, factor_m = layer_norm(mid)
    h_mlp = (normed_m * gain_two).astype(jnp.bfloat16)
    gate_up = apply_t(h_mlp, full_in, n_dp)
    hidden_out, glu_pull = jax.vjp(glu_piece, gate_up)
    hidden = hidden_out.astype(jnp.bfloat16)
    result = mid + apply_t(hidden, full_down, n_dp)
    output = result.astype(jnp.bfloat16)
    grad_down = grad_t(cotangent, hidden, n_dp)
    grad_hidden = apply_back(cotangent, full_down)
    grad_gate_up = glu_pull(grad_hidden)[0].astype(jnp.bfloat16)
    grad_inw = grad_t(grad_gate_up, h_mlp, n_dp)
    grad_hmlp = apply_back(grad_gate_up, full_in)
    grad_gain_two = jnp.sum(grad_hmlp * normed_m, axis=0)
    grad_mid = cotangent.astype(jnp.float32) + norm_back(grad_hmlp * gain_two, normed_m, factor_m)
    grad_branch = grad_mid.astype(jnp.bfloat16)
    grad_outw = grad_t(grad_branch, attn_out, n_dp)
    grad_attn = apply_back(grad_branch, full_out).astype(jnp.bfloat16)
    grad_query, grad_kv = attn_bwd(query, key_value, halo_lo, halo_hi, tag_query, wide_tag, grad_attn)
    grad_qkv = rope_bwd(grad_query, grad_kv, cosine, sine)
    grad_qkvw = grad_t(grad_qkv, h_attn, n_dp)
    grad_hattn = apply_back(grad_qkv, full_qkv)
    grad_gain_one = jnp.sum(grad_hattn * normed_a, axis=0)
    grad_tokens = grad_mid + norm_back(grad_hattn * gain_one, normed_a, factor_a)
    height = out_cols + in_cols + down_lines + qkv_cols + 8
    tail = 8 + (-height) % (RING_WAYS * 16)
    gain_both = jnp.concatenate(
        [
            gain_blocks(grad_gain_two, 1, n_seq, rows, 1)[0],
            gain_blocks(grad_gain_one, 1, n_seq, rows, tail - 1)[0],
        ],
        1,
    )
    blocks = jnp.stack(
        [
            jnp.concatenate(
                [
                    *lax.optimization_barrier(
                        (
                            grad_outw[d].reshape(n_seq, out_cols, rows),
                            grad_inw[d].reshape(n_seq, in_cols, rows),
                            grad_down[d]
                            .reshape(n_seq, down_cols, down_rows)
                            .reshape(n_seq, down_lines, rows),
                            grad_qkvw[d].reshape(n_seq, qkv_cols, rows),
                            gain_both,
                        )
                    ),
                ],
                1,
            )
            for d in range(n_dp)
        ]
    )
    depth = blocks.shape[2]
    half = lax.psum_scatter(
        blocks.reshape(n_dp, n_seq * depth, rows).astype(jnp.bfloat16),
        "dp",
        scatter_dimension=0,
        tiled=True,
    )
    late = ring_reduce(half.reshape(n_seq, depth, rows), order, RING_WAYS)
    at = 0
    late_out = late[at : at + out_cols].T
    at += out_cols
    late_in = late[at : at + in_cols].T
    at += in_cols
    late_down = late[at : at + down_lines].reshape(down_cols, down_rows).T
    at += down_lines
    late_qkv = late[at : at + qkv_cols].T
    at += qkv_cols
    late_gain_two = late[at, : gain_mlp.shape[0]]
    late_gain_one = late[at + 1, : gain_attn.shape[0]]
    return (
        output,
        grad_tokens,
        late_qkv,
        late_out,
        late_in,
        late_down,
        late_gain_one,
        late_gain_two,
    )


def solution(mesh):
    placed = (
        P(("dp", "seq"), None),
        P(("dp", "seq")),
        P(("dp", "seq")),
        P("dp", "seq"),
        P("dp", "seq"),
        P("dp", "seq"),
        P("dp", "seq"),
        P("seq"),
        P("seq"),
        P(("dp", "seq"), None),
    )
    return jax.shard_map(
        functools.partial(on_device, ring_order(mesh)),
        mesh=mesh,
        in_specs=placed,
        out_specs=(
            P(("dp", "seq"), None),
            P(("dp", "seq"), None),
            P("dp", "seq"),
            P("dp", "seq"),
            P("dp", "seq"),
            P("dp", "seq"),
            P("seq"),
            P("seq"),
        ),
        check_vma=False,
    )
```

profile of v0, /device:TPU:0, one launch (start us, length us, event | category | flops | bytes accessed | tf_op | source)
XLA Modules:
  0.0 422.5 jit_solution(1259422018765155763)
XLA Ops:
  7.9 1.6 pad_maximum_fusion.3
  11.8 3.4 concatenate.42
  16.1 4.8 %collective-permute-start = (s32[64]{0:T(128)S(1)}, s32[64]{0:T(128)S(1)}, u32[]{:S(2)}, u32[]{:S(2)}) collective-permute-start(s32[64]{0:T(128)S(1)} %get-tuple-element.67), channel_id=1, source_target_pairs={{0,1},{1,2},{2,3},{3,4},{4,5},{5,6},{6,7},{7,8},{8,9},{9,10},{10,1... | collective-permute-start | bytes 776 | tf_op jit(solution)/shard_map/ppermute | solution.py:25
  20.9 1.3 collective-permute-start.1
  23.2 2.4 copy.29.cos_ref
  25.6 2.0 tile.20
  27.6 3.6 copy.30.sin_ref
  32.6 46.0 %all-gather.3.cloned.1.call-done = bf16[6400,384]{1,0:T(8,128)(2,1)} async-done(((bf16[200,384]{1,0:T(8,128)(2,1)}), bf16[6400,384]{1,0:T(8,128)(2,1)}) %all-gather.3.cloned.1.call-update) | async-done | bytes 4915216 | tf_op jit(solution)/shard_map/all_gather | solution.py:506
  78.6 4.2 slice.123
  82.8 1.4 slice.124
  85.0 1.5 copy.41
  86.5 5.8 %copy.45 = bf16[2,384,2304]{2,1,0:T(8,128)(2,1)} copy(bf16[2,384,2304]{1,2,0:T(8,128)(2,1)} %bitcast.95) | data formatting | bytes 7077888 | tf_op jit(solution)/shard_map/tn,dnr->tdr/dot_general | solution.py:525
  92.9 1.2 copy-done.27
  94.0 8.2 %convolution_bitcast_fusion.1.qkv_ref = f32[1024,2304]{1,0:T(8,128)} fusion(bf16[2,2304,384]{2,1,0:T(8,128)(2,1)} %bitcast.96, bf16[128,2,8,384]{3,2,1,0:T(8,128)(2,1)S(1)} %bitcast.121), kind=kOutput, calls=%fused_computation.4 | convolution fusion | flops 3623878656 | bytes 14548992 | tf_op jit(solution)/shard_map/tdr,dnr->tn/dot_general | solution.py:521
  102.3 9.6 %shard_map.161 = (bf16[1024,768]{1,0:T(8,128)(2,1)}, bf16[1024,1536]{1,0:T(8,128)(2,1)}) custom-call(f32[1024,2304]{1,0:T(8,128)} %convolution_bitcast_fusion.1.qkv_ref, f32[1024,768]{1,0:T(8,128)} %copy.29.cos_ref, f32[1024,768]{1,0:T(8,128)} %copy.30.sin_ref), custom_call_target="tpu_custom_call" | custom-call | tf_op jit(solution)/shard_map/pallas_call | solution.py:464
  111.9 1.4 copy-done
  113.3 25.0 %shard_map.162 = (bf16[1024,768]{1,0:T(8,128)(2,1)S(1)}, bf16[64,1536]{1,0:T(8,128)(2,1)S(1)}, bf16[64,1536]{1,0:T(8,128)(2,1)S(1)}) custom-call(bf16[1024,768]{1,0:T(8,128)(2,1)S(1)} %copy-done, bf16[1024,1536]{1,0:T(8,128)(2,1)} %get-tuple-element.28.kv_ref, s32[1024,1]{1,0:T(8,128)S(1)} %copy.31.tq_ref, s32[1,1152]{1,0:T(1,128)S(1)} %reshape.172.tk_ref), custom_call_target="tpu_custom_call" | custom-call | tf_op jit(solution)/shard_map/pallas_call | solution.py:382
  138.3 3.1 convert_add_fusion
  141.4 10.1 %all-gather.5.cloned.1.call-done = bf16[7168,384]{1,0:T(8,128)(2,1)} async-done(((bf16[224,384]{1,0:T(8,128)(2,1)}), bf16[7168,384]{1,0:T(8,128)(2,1)}) %all-gather.5.cloned.1.call-update) | async-done | bytes 5505040 | tf_op jit(solution)/shard_map/all_gather | solution.py:506
  152.3 4.3 %slice.102 = bf16[2,16,144,384]{3,2,1,0:T(8,128)(2,1)} slice(bf16[2,16,224,384]{3,2,1,0:T(8,128)(2,1)} %bitcast.101), slice={[0:2], [0:16], [0:144], [0:384]} | slice | bytes 7077888 | tf_op jit(solution)/shard_map/slice | solution.py:577
  156.6 1.3 fusion.50
  157.9 2.4 slice.105
  160.3 2.1 reduce_sum.92
  162.5 2.4 multiply_reduce_fusion.2
  164.9 1.6 maximum_maximum_fusion
  166.7 4.5 %fusion.27 = f32[2,576,1024]{2,1,0:T(8,128)} fusion(bf16[2,768,576]{2,1,0:T(8,128)(2,1)S(1)} %bitcast.115, bf16[1024,768]{1,0:T(8,128)(2,1)S(1)} %copy-done.24), kind=kOutput, calls=%fused_computation.61 | convolution fusion | flops 1811939328 | bytes 8060928 | tf_op jit(solution)/shard_map/tn,dnr->tdr/dot_general | solution.py:525
  171.2 6.1 %copy.37 = f32[1024,1152]{1,0:T(8,128)} copy(f32[1024,1152]{0,1:T(8,128)} %bitcast.104) | data formatting | bytes 9437184 | tf_op jit(solution)/shard_map/reshape | solution.py:526
  177.3 2.5 multiply_convert_fusion.1
  179.8 5.9 %convolution_bitcast_fusion = f32[1024,2304]{1,0:T(8,128)S(1)} fusion(bf16[2,2304,384]{2,1,0:T(8,128)(2,1)} %bitcast.93, bf16[128,2,8,384]{3,2,1,0:T(8,128)(2,1)S(1)} %bitcast.122), kind=kOutput, calls=%fused_computation.3 | convolution fusion | flops 3623878656 | bytes 14548992 | tf_op jit(solution)/shard_map/tdr,dnr->tn/dot_general | solution.py:521
  185.8 11.3 %fusion.29 = (f32[1024,1152]{1,0:T(8,128)}, f32[1024,1152]{1,0:T(8,128)S(1)}) fusion(f32[1024,1152]{1,0:T(8,128)S(1)} %bitcast.92, f32[1024,2304]{1,0:T(8,128)S(1)} %convolution_bitcast_fusion), kind=kLoop, calls=%fused_computation.65 | loop fusion | flops 76677120 | bytes 18874368 | tf_op jit(solution)/shard_map/transpose(jvp())/mul | solution.py:80
  197.1 3.5 multiply_add_fusion
  200.6 8.0 %fusion.38 = bf16[2304,384]{1,0:T(8,128)(2,1)} fusion(bf16[1024,768]{1,0:T(8,128)(2,1)S(1)} %multiply_convert_fusion.1, f32[1024,1152]{1,0:T(8,128)S(1)} %get-tuple-element.54, f32[1024,1152]{1,0:T(8,128)} %get-tuple-element.52), kind=kOutput, calls=%fused_computation.76 | convolution fusion | flops 1816657920 | bytes 11993088 | tf_op jit(solution)/shard_map/dot_general | solution.py:532
  208.6 3.8 fusion.34
  212.4 5.8 %copy.39 = bf16[2,384,2304]{2,1,0:T(8,128)(2,1)} copy(bf16[2,384,2304]{1,2,0:T(8,128)(2,1)} %bitcast.94) | data formatting | bytes 7077888 | tf_op jit(solution)/shard_map/tn,dnr->tdr/dot_general | solution.py:525
  218.2 10.2 %multiply_reduce_fusion = (bf16[768]{0:T(1024)(128)(2,1)S(1)}, f32[1024]{0:T(1024)S(1)}, f32[1024]{0:T(1024)S(1)}, f32[1024,768]{1,0:T(8,128)S(1)}) fusion(f32[1024,768]{1,0:T(8,128)} %convert_add_fusion, f32[1024]{0:T(1024)S(1)} %add_rsqrt_fusion, f32[1024]{0:T(1024)S(1)} %broadcast_multiply_fusion.4, f32[768]{0:T(1024)S(1)} %reshape.192, ...), kind=kOutput, calls=%fused_computation.41 | convolution fusion | flops 3634885888 | bytes 19288576 | tf_op jit(solution)/shard_map/tn,dnr->tdr/dot_general | solution.py:525
  228.4 1.7 multiply_add_fusion.1
  230.1 1.9 fusion.42
  232.0 1.0 fusion.40
  233.0 1.4 convolution_convert_fusion.do_ref
  234.5 41.4 %shard_map.163 = (f32[1024,768]{1,0:T(8,128)}, f32[1024,1536]{1,0:T(8,128)}) custom-call(bf16[1024,768]{1,0:T(8,128)(2,1)S(1)} %copy-done.1, bf16[1024,1536]{1,0:T(8,128)(2,1)} %get-tuple-element.28.kv_ref, bf16[64,1536]{1,0:T(8,128)(2,1)S(1)} %get-tuple-element.32.lo_ref, bf16[64,1536]{1,0:T(8,128)(2,1)S(1)} %get-tuple-element.33.hi_ref, ...), custom_call_target="tpu_custom_call" | custom-call | tf_op jit(solution)/shard_map/pallas_call | solution.py:401
  275.9 9.8 %shard_map.164 = bf16[1024,2304]{1,0:T(8,128)(2,1)} custom-call(f32[1024,768]{1,0:T(8,128)} %get-tuple-element.34.dq_ref, f32[1024,1536]{1,0:T(8,128)} %get-tuple-element.35.dkv_ref, f32[1024,768]{1,0:T(8,128)} %copy.29.cos_ref, f32[1024,768]{1,0:T(8,128)} %copy.30.sin_ref), custom_call_target="tpu_custom_call" | custom-call | tf_op jit(solution)/shard_map/pallas_call | solution.py:478
  285.8 6.4 %fusion.36 = bf16[2304,384]{1,0:T(8,128)(2,1)} fusion(bf16[1024,2304]{1,0:T(8,128)(2,1)} %shard_map.164, bf16[1024,768]{1,0:T(8,128)(2,1)S(1)} %copy-done.28), kind=kOutput, calls=%fused_computation.74 | convolution fusion | flops 1811939328 | bytes 7274496 | tf_op jit(solution)/shard_map/dot_general | solution.py:532
  292.1 4.0 fusion.32
  296.2 1.1 convolution_bitcast_fusion.3
  297.3 2.3 convolution_bitcast_fusion.2
  300.0 5.9 %fusion.18 = (bf16[768]{0:T(1024)(128)(2,1)S(1)}, f32[1024]{0:T(1024)S(1)}, f32[1024]{0:T(1024)S(1)}, f32[1024,768]{1,0:T(8,128)}) fusion(bf16[1024,768]{1,0:T(8,128)(2,1)S(1)} %copy-done.9, f32[1024]{0:T(1024)S(1)} %add_rsqrt_fusion.1, f32[1024]{0:T(1024)S(1)} %broadcast_multiply_fusion.5, f32[768]{0:T(1024)S(1)} %reshape.191, ...), kind=kOutput, calls=%fused_computation.37 | convolution fusion | flops 3630953728 | bytes 12997120 | tf_op jit(solution)/shard_map/tn,dnr->tdr/dot_general | solution.py:525
  306.7 1.4 reshape_reshape.6
  309.1 1.8 copy.50
  310.9 1.4 reshape_reshape.7
  313.2 2.9 convert_dynamic-update-slice_fusion.3
  316.1 1.0 convert_dynamic-update-slice_fusion.5
  317.1 1.4 convert_dynamic-update-slice_fusion.2
  319.3 1.5 convert_dynamic-update-slice_fusion.1
  320.7 1.0 convert_dynamic-update-slice_fusion.4
  321.8 1.5 convert_dynamic-update-slice_fusion
  323.9 9.0 %pad_maximum_fusion = bf16[2,6656,384]{2,1,0:T(8,128)(2,1)} fusion(bf16[1,6656,384]{2,1,0:T(8,128)(2,1)} %bitcast.37, bf16[1,6656,384]{2,1,0:T(8,128)(2,1)} %bitcast.99), kind=kLoop, calls=%fused_computation | loop fusion | flops 5111808 | bytes 20447232 | tf_op jit(solution)/shard_map/stack | solution.py:616
  333.0 4.4 %copy.34 = bf16[1024,1152]{0,1:T(8,128)(2,1)} copy(bf16[1024,1152]{1,0:T(8,128)(2,1)} %get-tuple-element.55) | data formatting | bytes 4718592 | tf_op jit(solution)/shard_map/convert_element_type | solution.py:588
  337.4 4.4 %fusion.17 = f32[1024,768]{1,0:T(8,128)} fusion(f32[1024,768]{1,0:T(8,128)S(1)} %copy-done.4, bf16[1024,768]{1,0:T(8,128)(2,1)} %param.10, f32[1024,768]{1,0:T(8,128)} %get-tuple-element.72, f32[1024]{0:T(1024)S(1)} %broadcast_multiply_fusion, f32[1024]{0:T(1024)S(1)} %broadcast_multiply_fusion.1, f32[768]{0:T(1024)S(1)} %reshape.191, ...), kind=kLoop, calls=%fused_computation.36 | loop fusion | flops 7077888 | bytes 11029504 | tf_op jit(solution)/shard_map/add | solution.py:606
  342.7 1.2 copy-done.18
  344.0 1.1 copy-done.20
  345.0 3.5 fusion.20
  348.5 1.8 reduce-scatter.2.cloned.1.call-done
  350.3 2.4 copy-done.2
  352.8 60.1 %shard_map.165 = f32[416,384]{1,0:T(8,128)S(1)} custom-call(bf16[16,416,384]{2,1,0:T(8,128)(2,1)S(1)} %bitcast.89), custom_call_target="tpu_custom_call" | custom-call | tf_op jit(solution)/shard_map/pallas_call | solution.py:210
  (119 shorter events, 16.7 us)
Async XLA Ops:
  7.2 71.4 %all-gather.3.cloned.1.call-start = ((), (), s32[]{:S(2)}) async-start(), calls=%async_computation.1 | async-start | bytes 5068800 | tf_op jit(solution)/shard_map/all_gather | solution.py:506
  9.5 142.0 %all-gather.5.cloned.1.call-start = ((), (), s32[]{:S(2)}) async-start(), calls=%async_computation.2 | async-start | bytes 5677056 | tf_op jit(solution)/shard_map/all_gather | solution.py:506
  15.2 335.1 %reduce-scatter.2.cloned.1.call-start = ((), (), s32[]{:S(2)}) async-start(), calls=%async_computation.3 | async-start | bytes 15335424 | tf_op jit(solution)/shard_map/reduce_scatter | solution.py:638
  16.1 16.4 %collective-permute-start = (s32[64]{0:T(128)S(1)}, s32[64]{0:T(128)S(1)}, u32[]{:S(2)}, u32[]{:S(2)}) collective-permute-start(s32[64]{0:T(128)S(1)} %get-tuple-element.67), channel_id=1, source_target_pairs={{0,1},{1,2},{2,3},{3,4},{4,5},{5,6},{6,7},{7,8},{8,9},{9,10},{10,1... | collective-permute-start | bytes 776 | tf_op jit(solution)/shard_map/ppermute | solution.py:25
  20.9 11.6 %collective-permute-start.1 = (s32[64]{0:T(128)S(1)}, s32[64]{0:T(128)S(1)}, u32[]{:S(2)}, u32[]{:S(2)}) collective-permute-start(s32[64]{0:T(128)S(1)} %get-tuple-element.66), channel_id=1, source_target_pairs={{1,0},{2,1},{3,2},{4,3},{5,4},{6,5},{7,6},{8,7},{9,8},{10,9},{11,1... | collective-permute-start | bytes 776 | tf_op jit(solution)/shard_map/ppermute | solution.py:26
  27.6 3.6 copy-start.7
  84.2 8.2 %copy-start.13 = (bf16[2,16,48,384]{3,2,1,0:T(8,128)(2,1)}, bf16[2,16,48,384]{3,2,1,0:T(8,128)(2,1)S(1)}, u32[]{:S(2)}) copy-start(bf16[2,16,48,384]{3,2,1,0:T(8,128)(2,1)S(1)} %slice.124) | copy-start | bytes 3538948
  92.9 1.2 copy-start.27
  111.9 1.4 copy-start
  113.3 25.0 %copy-start.8 = (bf16[1024,768]{1,0:T(8,128)(2,1)S(1)}, bf16[1024,768]{1,0:T(8,128)(2,1)}, u32[]{:S(2)}) copy-start(bf16[1024,768]{1,0:T(8,128)(2,1)} %param.10) | copy-start | bytes 4718596
  113.3 25.0 %copy-start.14 = (bf16[2,16,48,384]{3,2,1,0:T(8,128)(2,1)S(1)}, bf16[2,16,48,384]{3,2,1,0:T(8,128)(2,1)}, u32[]{:S(2)}) copy-start(bf16[2,16,48,384]{3,2,1,0:T(8,128)(2,1)} %copy-done.13) | copy-start | bytes 3538948
  164.9 1.8 copy-start.24
  166.5 4.7 %copy-start.19 = (bf16[2,16,48,576]{3,2,1,0:T(8,128)(2,1)}, bf16[2,16,48,576]{3,2,1,0:T(8,128)(2,1)S(1)}, u32[]{:S(2)}) copy-start(bf16[2,16,48,576]{3,2,1,0:T(8,128)(2,1)S(1)} %maximum_maximum_fusion) | copy-start | bytes 5308420
  177.3 8.4 %slice-start = ((s8[4718592]{0:T(1024)(128)(4,1)}), s8[4194304]{0:T(1024)(128)(4,1)S(1)}, s32[]{:S(2)}) async-start(s8[4718592]{0:T(1024)(128)(4,1)} %bitcast.91), calls=%async_computation.4 | async-start | bytes 8388608
  179.8 6.0 %slice-start.1 = ((s8[4718592]{0:T(1024)(128)(4,1)}), s8[524288]{0:T(1024)(128)(4,1)S(1)}, s32[]{:S(2)}) async-start(s8[4718592]{0:T(1024)(128)(4,1)} %bitcast.91), calls=%async_computation.5 | async-start | bytes 1048576
  200.6 8.0 %copy-start.11 = (f32[1024,1152]{1,0:T(8,128)}, f32[1024,1152]{1,0:T(8,128)S(1)}, u32[]{:S(2)}) copy-start(f32[1024,1152]{1,0:T(8,128)S(1)} %get-tuple-element.54) | copy-start | bytes 14155780
  200.6 8.0 %copy-start.15 = (f32[1024,1152]{1,0:T(8,128)S(1)}, f32[1024,1152]{1,0:T(8,128)}, u32[]{:S(2)}) copy-start(f32[1024,1152]{1,0:T(8,128)} %get-tuple-element.52) | copy-start | bytes 14155780
  218.2 10.2 %copy-start.5 = (f32[1024,768]{1,0:T(8,128)S(1)}, f32[1024,768]{1,0:T(8,128)}, u32[]{:S(2)}) copy-start(f32[1024,768]{1,0:T(8,128)} %convert_add_fusion) | copy-start | bytes 9437188
  218.2 10.2 %copy-start.25 = (bf16[1024,768]{1,0:T(8,128)(2,1)S(1)}, bf16[1024,768]{1,0:T(8,128)(2,1)}, u32[]{:S(2)}) copy-start(bf16[1024,768]{1,0:T(8,128)(2,1)} %param.19) | copy-start | bytes 4718596
  230.1 2.9 copy-start.3
  230.1 2.9 copy-start.29
  233.0 1.5 copy-start.1
  275.9 9.8 %copy-start.28 = (bf16[1024,768]{1,0:T(8,128)(2,1)S(1)}, bf16[1024,768]{1,0:T(8,128)(2,1)}, u32[]{:S(2)}) copy-start(bf16[1024,768]{1,0:T(8,128)(2,1)} %copy-done.27) | copy-start | bytes 4718596
  285.8 6.4 %copy-start.12 = (bf16[1024,2304]{1,0:T(8,128)(2,1)S(1)}, bf16[1024,2304]{1,0:T(8,128)(2,1)}, u32[]{:S(2)}) copy-start(bf16[1024,2304]{1,0:T(8,128)(2,1)} %shard_map.164) | copy-start | bytes 14155780
  292.1 4.0 copy-start.10
  292.1 4.0 copy-start.26
  297.3 2.4 copy-start.9
  297.3 2.6 copy-start.16
  305.8 2.4 copy-start.17
  312.3 4.9 %copy-start.23 = (bf16[2304,384]{1,0:T(8,128)(2,1)S(1)}, bf16[2304,384]{1,0:T(8,128)(2,1)}, u32[]{:S(2)}) copy-start(bf16[2304,384]{1,0:T(8,128)(2,1)} %fusion.36) | copy-start | bytes 5308420
  316.1 3.2 copy-start.21
  318.6 3.2 copy-start.22
  333.0 4.4 %copy-start.4 = (f32[1024,768]{1,0:T(8,128)S(1)}, f32[1024,768]{1,0:T(8,128)}, u32[]{:S(2)}) copy-start(f32[1024,768]{1,0:T(8,128)} %copy-done.3) | copy-start | bytes 9437188
  337.4 5.3 %copy-start.6 = (f32[1024,768]{1,0:T(8,128)S(1)}, f32[1024,768]{1,0:T(8,128)}, u32[]{:S(2)}) copy-start(f32[1024,768]{1,0:T(8,128)} %convert_add_fusion) | copy-start | bytes 9437188
  337.4 6.5 %copy-start.18 = (bf16[1024,1152]{0,1:T(8,128)(2,1)S(1)}, bf16[1024,1152]{0,1:T(8,128)(2,1)}, u32[]{:S(2)}) copy-start(bf16[1024,1152]{0,1:T(8,128)(2,1)} %copy.34) | copy-start | bytes 7077892
  337.4 7.6 %copy-start.20 = (bf16[2,16,48,576]{3,2,1,0:T(8,128)(2,1)S(1)}, bf16[2,16,48,576]{3,2,1,0:T(8,128)(2,1)}, u32[]{:S(2)}) copy-start(bf16[2,16,48,576]{3,2,1,0:T(8,128)(2,1)} %copy-done.19) | copy-start | bytes 5308420
  350.3 2.4 copy-start.2
Sparse Core Ops, SparseCore 0:
  11.4 67.1 all-gather.2
  82.0 69.4 all-gather.4
  333.1 17.2 reduce-scatter.1
where the time goes:
time: 430 us; the launch traced here: 423 us
  Pallas kernels  146 us (34%)
  local copies, waits for them, and re-layouts  81.8 us (19%)
  matrix products  71.4 us (17%)
  waiting for transfers between devices  58 us (13%)
  other arithmetic  44.5 us (10%)
  between operations  14.7 us (3%)
  starting transfers between devices  6.24 us (1%)
    pallas_call x1, Pallas kernels, ring_reduce(): pl.pallas_call(functools.partial(ring_kernel, tuple(order), per_way), out...  60.1 us
    all_gather x2, waiting for transfers between devices, gather_rows(): every = lax.all_gather(payload, ('dp', 'seq'), axis=0, tiled=True)  56.1 us
    pallas_call x1, Pallas kernels, attn_bwd(): pl.pallas_call(attn_bwd_kernel, out_shape=(jax.ShapeDtypeStruct((count, w...  41.4 us
    dot_general x8, matrix products, grad_t(): lax.dot_general(grad, left[:, d * width:(d + 1) * width], (((0,), (0,)),...  28.6 us
    pallas_call x1, Pallas kernels, attn_fwd(): pl.pallas_call(attn_fwd_kernel, out_shape=(jax.ShapeDtypeStruct((count, w...  25 us
    dot_general x4, matrix products, apply_back(): jnp.einsum('tn,dnr->tdr', grad, weight_t, preferred_element_type=jnp.floa...  22 us
    dot_general x4, matrix products, apply_t(): jnp.einsum('tdr,dnr->tn', front(left, n_dp), weight_t, preferred_element_...  20.8 us
    unnamed x72, local copies, waits for them, and re-layouts  19.9 us
  transfers between devices with their start and end apart: 5, of which 3 were waited for; matrix products, arithmetic and copies ran while one was open for 13% of the time, Pallas kernels for 8%

commit v1 on v0

--- a/solution.py
+++ b/solution.py
@@ -317,8 +317,8 @@
     to_after.wait_send()
 
 
-def attn_bwd_kernel(q_ref, kv_ref, lo_ref, hi_ref, tq_ref, tk_ref, do_ref, dq_ref, dkv_ref,
-                    wide, dwide, send_lo, send_hi, recv_lo, recv_hi, send_sem, recv_sem):
+def attn_bwd_kernel(q_ref, kv_ref, lo_ref, hi_ref, tq_ref, tk_ref, do_ref, cos_ref, sin_ref, g_ref,
+                    dq_ref, wide, dwide, send_lo, send_hi, recv_lo, recv_hi, send_sem, recv_sem):
     width = q_ref.shape[1]
     count = q_ref.shape[0]
     blocks = count // QB
@@ -363,11 +363,21 @@
     to_before.start()
     to_after.start()
     lax.fori_loop(1, blocks - 1, block, 0)
-    dkv_ref[...] = dwide[pl.ds(HALF, count), :]
     to_before.wait_recv()
     to_after.wait_recv()
-    dkv_ref[pl.ds(0, HALF), :] += recv_lo[...].astype(jnp.float32)
-    dkv_ref[pl.ds(count - HALF, HALF), :] += recv_hi[...].astype(jnp.float32)
+    dwide[pl.ds(HALF, HALF), :] += recv_lo[...].astype(jnp.float32)
+    dwide[pl.ds(count, HALF), :] += recv_hi[...].astype(jnp.float32)
+    for chunk in range(count // ROPE_ROWS):
+        r0 = chunk * ROPE_ROWS
+        c = cos_ref[pl.ds(r0, ROPE_ROWS), :]
+        s = sin_ref[pl.ds(r0, ROPE_ROWS), :]
+        dq = dq_ref[pl.ds(r0, ROPE_ROWS), :]
+        dk = dwide[pl.ds(HALF + r0, ROPE_ROWS), pl.ds(0, width)]
+        g_ref[pl.ds(r0, ROPE_ROWS), pl.ds(0, width)] = (dq * c - head_rotate(dq) * s).astype(g_ref.dtype)
+        g_ref[pl.ds(r0, ROPE_ROWS), pl.ds(width, width)] = (dk * c - head_rotate(dk) * s).astype(g_ref.dtype)
+        g_ref[pl.ds(r0, ROPE_ROWS), pl.ds(2 * width, width)] = dwide[
+            pl.ds(HALF + r0, ROPE_ROWS), pl.ds(width, width)
+        ].astype(g_ref.dtype)
     to_before.wait_send()
     to_after.wait_send()
 
@@ -395,18 +405,16 @@
     )(query, kv, tag_q.reshape(count, 1), tag_k.reshape(1, -1))
 
 
-def attn_bwd(query, kv, lo, hi, tag_q, tag_k, grad_out):
+def attn_bwd(query, kv, lo, hi, tag_q, tag_k, grad_out, cosine, sine):
     count, width = query.shape
     vm = pl.BlockSpec(memory_space=pltpu.VMEM)
     return pl.pallas_call(
         attn_bwd_kernel,
-        out_shape=(
-            jax.ShapeDtypeStruct((count, width), jnp.float32),
-            jax.ShapeDtypeStruct(kv.shape, jnp.float32),
-        ),
-        in_specs=[vm] * 7,
-        out_specs=(vm, vm),
+        out_shape=jax.ShapeDtypeStruct((count, 3 * width), jnp.bfloat16),
+        in_specs=[vm] * 9,
+        out_specs=vm,
         scratch_shapes=[
+            pltpu.VMEM((count, width), jnp.float32),
             pltpu.VMEM((count + 2 * HALF, kv.shape[1]), kv.dtype),
             pltpu.VMEM((count + 2 * HALF, kv.shape[1]), jnp.float32),
             pltpu.VMEM((HALF, kv.shape[1]), jnp.bfloat16),
@@ -419,7 +427,7 @@
         compiler_params=pltpu.CompilerParams(
             collective_id=3, has_side_effects=True, vmem_limit_bytes=VMEM_LIMIT
         ),
-    )(query, kv, lo, hi, tag_q.reshape(count, 1), tag_k.reshape(1, -1), grad_out)
+    )(query, kv, lo, hi, tag_q.reshape(count, 1), tag_k.reshape(1, -1), grad_out, cosine, sine)
 
 
 ROPE_ROWS = 256
@@ -598,8 +606,9 @@
     grad_branch = grad_mid.astype(jnp.bfloat16)
     grad_outw = grad_t(grad_branch, attn_out, n_dp)
     grad_attn = apply_back(grad_branch, full_out).astype(jnp.bfloat16)
-    grad_query, grad_kv = attn_bwd(query, key_value, halo_lo, halo_hi, tag_query, wide_tag, grad_attn)
-    grad_qkv = rope_bwd(grad_query, grad_kv, cosine, sine)
+    grad_qkv = attn_bwd(
+        query, key_value, halo_lo, halo_hi, tag_query, wide_tag, grad_attn, cosine, sine
+    )
     grad_qkvw = grad_t(grad_qkv, h_attn, n_dp)
     grad_hattn = apply_back(grad_qkv, full_qkv)
     grad_gain_one = jnp.sum(grad_hattn * normed_a, axis=0)

time: 430 us -> 424 us (0.986)
  Pallas kernels: 146 us -> 141 us
    pallas_call x2 -> x1, Pallas kernels: 51.2 us -> 46.3 us  [attn_bwd(): pl.pallas_call(attn_bwd_kernel, out_shape=jax.ShapeDtypeStruct((count, 3...]
    unnamed x72 -> x70, local copies, waits for them, and re-layouts: 19.9 us -> 19.5 us
where the time goes in v1:
time: 424 us; the launch traced here: 417 us
  Pallas kernels  141 us (33%)
  local copies, waits for them, and re-layouts  81.1 us (19%)
  matrix products  71.5 us (17%)
  waiting for transfers between devices  58.2 us (14%)
  other arithmetic  44.9 us (11%)
  between operations  14.5 us (3%)
  starting transfers between devices  6.24 us (1%)
    pallas_call x1, Pallas kernels, ring_reduce(): pl.pallas_call(functools.partial(ring_kernel, tuple(order), per_way), out...  60.1 us
    all_gather x2, waiting for transfers between devices, gather_rows(): every = lax.all_gather(payload, ('dp', 'seq'), axis=0, tiled=True)  56.3 us
    pallas_call x1, Pallas kernels, attn_bwd(): pl.pallas_call(attn_bwd_kernel, out_shape=jax.ShapeDtypeStruct((count, 3...  46.3 us
    dot_general x8, matrix products, grad_t(): lax.dot_general(grad, left[:, d * width:(d + 1) * width], (((0,), (0,)),...  28.7 us
    pallas_call x1, Pallas kernels, attn_fwd(): pl.pallas_call(attn_fwd_kernel, out_shape=(jax.ShapeDtypeStruct((count, w...  24.8 us
    dot_general x4, matrix products, apply_back(): jnp.einsum('tn,dnr->tdr', grad, weight_t, preferred_element_type=jnp.floa...  22 us
    dot_general x4, matrix products, apply_t(): jnp.einsum('tdr,dnr->tn', front(left, n_dp), weight_t, preferred_element_...  20.7 us
    unnamed x70, local copies, waits for them, and re-layouts  19.5 us
  transfers between devices with their start and end apart: 5, of which 3 were waited for; matrix products, arithmetic and copies ran while one was open for 13% of the time, Pallas kernels for 8%

profile of v1, /device:TPU:0, one launch (start us, length us, event | category | flops | bytes accessed | tf_op | source)
XLA Modules:
  0.0 417.4 jit_solution(9974704588528904903)
XLA Ops:
  7.9 1.6 pad_maximum_fusion.3
  11.8 3.4 concatenate.42
  16.1 4.8 %collective-permute-start = (s32[64]{0:T(128)S(1)}, s32[64]{0:T(128)S(1)}, u32[]{:S(2)}, u32[]{:S(2)}) collective-permute-start(s32[64]{0:T(128)S(1)} %get-tuple-element.63), channel_id=1, source_target_pairs={{0,1},{1,2},{2,3},{3,4},{4,5},{5,6},{6,7},{7,8},{8,9},{9,10},{10,1... | collective-permute-start | bytes 776 | tf_op jit(solution)/shard_map/ppermute | solution.py:25
  20.9 1.3 collective-permute-start.1
  23.2 2.4 copy.29.cos_ref
  25.6 2.0 tile.20
  27.6 3.6 copy.30.sin_ref
  32.6 46.0 %all-gather.3.cloned.1.call-done = bf16[6400,384]{1,0:T(8,128)(2,1)} async-done(((bf16[200,384]{1,0:T(8,128)(2,1)}), bf16[6400,384]{1,0:T(8,128)(2,1)}) %all-gather.3.cloned.1.call-update) | async-done | bytes 4915216 | tf_op jit(solution)/shard_map/all_gather | solution.py:514
  78.6 4.2 %slice.123 = bf16[2,16,144,384]{3,2,1,0:T(8,128)(2,1)} slice(bf16[2,16,200,384]{3,2,1,0:T(8,128)(2,1)} %bitcast.107), slice={[0:2], [0:16], [0:144], [0:384]} | slice | bytes 7077888 | tf_op jit(solution)/shard_map/slice | solution.py:565
  82.7 1.4 slice.124
  85.0 1.4 copy.41
  86.5 5.9 %copy.45 = bf16[2,384,2304]{2,1,0:T(8,128)(2,1)} copy(bf16[2,384,2304]{1,2,0:T(8,128)(2,1)} %bitcast.95) | data formatting | bytes 7077888 | tf_op jit(solution)/shard_map/tn,dnr->tdr/dot_general | solution.py:533
  92.9 1.2 copy-done.26
  94.0 8.2 %convolution_bitcast_fusion.1.qkv_ref = f32[1024,2304]{1,0:T(8,128)} fusion(bf16[2,2304,384]{2,1,0:T(8,128)(2,1)} %bitcast.96, bf16[128,2,8,384]{3,2,1,0:T(8,128)(2,1)S(1)} %bitcast.121), kind=kOutput, calls=%fused_computation.4 | convolution fusion | flops 3623878656 | bytes 14548992 | tf_op jit(solution)/shard_map/tdr,dnr->tn/dot_general | solution.py:529
  102.3 9.8 %shard_map.161 = (bf16[1024,768]{1,0:T(8,128)(2,1)}, bf16[1024,1536]{1,0:T(8,128)(2,1)}) custom-call(f32[1024,2304]{1,0:T(8,128)} %convolution_bitcast_fusion.1.qkv_ref, f32[1024,768]{1,0:T(8,128)} %copy.29.cos_ref, f32[1024,768]{1,0:T(8,128)} %copy.30.sin_ref), custom_call_target="tpu_custom_call" | custom-call | tf_op jit(solution)/shard_map/pallas_call | solution.py:472
  112.1 1.4 copy-done
  113.5 24.8 %shard_map.162 = (bf16[1024,768]{1,0:T(8,128)(2,1)S(1)}, bf16[64,1536]{1,0:T(8,128)(2,1)S(1)}, bf16[64,1536]{1,0:T(8,128)(2,1)S(1)}) custom-call(bf16[1024,768]{1,0:T(8,128)(2,1)S(1)} %copy-done, bf16[1024,1536]{1,0:T(8,128)(2,1)} %get-tuple-element.26.kv_ref, s32[1024,1]{1,0:T(8,128)S(1)} %copy.31.tq_ref, s32[1,1152]{1,0:T(1,128)S(1)} %reshape.172.tk_ref), custom_call_target="tpu_custom_call" | custom-call | tf_op jit(solution)/shard_map/pallas_call | solution.py:392
  138.3 3.1 convert_add_fusion
  141.5 10.3 %all-gather.5.cloned.1.call-done = bf16[7168,384]{1,0:T(8,128)(2,1)} async-done(((bf16[224,384]{1,0:T(8,128)(2,1)}), bf16[7168,384]{1,0:T(8,128)(2,1)}) %all-gather.5.cloned.1.call-update) | async-done | bytes 5505040 | tf_op jit(solution)/shard_map/all_gather | solution.py:514
  152.6 4.2 %slice.102 = bf16[2,16,144,384]{3,2,1,0:T(8,128)(2,1)} slice(bf16[2,16,224,384]{3,2,1,0:T(8,128)(2,1)} %bitcast.101), slice={[0:2], [0:16], [0:144], [0:384]} | slice | bytes 7077888 | tf_op jit(solution)/shard_map/slice | solution.py:585
  156.8 1.3 fusion.50
  158.1 2.4 slice.105
  160.6 2.1 reduce_sum.92
  162.7 2.4 multiply_reduce_fusion.2
  165.1 1.6 maximum_maximum_fusion
  166.9 4.5 %fusion.27 = f32[2,576,1024]{2,1,0:T(8,128)} fusion(bf16[2,768,576]{2,1,0:T(8,128)(2,1)S(1)} %bitcast.115, bf16[1024,768]{1,0:T(8,128)(2,1)S(1)} %copy-done.24), kind=kOutput, calls=%fused_computation.61 | convolution fusion | flops 1811939328 | bytes 8060928 | tf_op jit(solution)/shard_map/tn,dnr->tdr/dot_general | solution.py:533
  171.4 6.2 %copy.37 = f32[1024,1152]{1,0:T(8,128)} copy(f32[1024,1152]{0,1:T(8,128)} %bitcast.104) | data formatting | bytes 9437184 | tf_op jit(solution)/shard_map/reshape | solution.py:534
  177.6 2.5 multiply_convert_fusion.1
  180.1 5.9 %convolution_bitcast_fusion = f32[1024,2304]{1,0:T(8,128)S(1)} fusion(bf16[2,2304,384]{2,1,0:T(8,128)(2,1)} %bitcast.93, bf16[128,2,8,384]{3,2,1,0:T(8,128)(2,1)S(1)} %bitcast.122), kind=kOutput, calls=%fused_computation.3 | convolution fusion | flops 3623878656 | bytes 14548992 | tf_op jit(solution)/shard_map/tdr,dnr->tn/dot_general | solution.py:529
  186.1 11.4 %fusion.29 = (f32[1024,1152]{1,0:T(8,128)}, f32[1024,1152]{1,0:T(8,128)S(1)}) fusion(f32[1024,1152]{1,0:T(8,128)S(1)} %bitcast.92, f32[1024,2304]{1,0:T(8,128)S(1)} %convolution_bitcast_fusion), kind=kLoop, calls=%fused_computation.65 | loop fusion | flops 76677120 | bytes 18874368 | tf_op jit(solution)/shard_map/transpose(jvp())/mul | solution.py:80
  197.4 3.5 multiply_add_fusion
  200.9 8.0 %fusion.38 = bf16[2304,384]{1,0:T(8,128)(2,1)} fusion(bf16[1024,768]{1,0:T(8,128)(2,1)S(1)} %multiply_convert_fusion.1, f32[1024,1152]{1,0:T(8,128)S(1)} %get-tuple-element.50, f32[1024,1152]{1,0:T(8,128)} %get-tuple-element.48), kind=kOutput, calls=%fused_computation.76 | convolution fusion | flops 1816657920 | bytes 11993088 | tf_op jit(solution)/shard_map/dot_general | solution.py:540
  208.9 3.8 fusion.34
  212.7 5.8 %copy.39 = bf16[2,384,2304]{2,1,0:T(8,128)(2,1)} copy(bf16[2,384,2304]{1,2,0:T(8,128)(2,1)} %bitcast.94) | data formatting | bytes 7077888 | tf_op jit(solution)/shard_map/tn,dnr->tdr/dot_general | solution.py:533
  218.5 10.2 %multiply_reduce_fusion = (bf16[768]{0:T(1024)(128)(2,1)S(1)}, f32[1024]{0:T(1024)S(1)}, f32[1024]{0:T(1024)S(1)}, f32[1024,768]{1,0:T(8,128)S(1)}) fusion(f32[1024,768]{1,0:T(8,128)} %convert_add_fusion, f32[1024]{0:T(1024)S(1)} %add_rsqrt_fusion, f32[1024]{0:T(1024)S(1)} %broadcast_multiply_fusion.4, f32[768]{0:T(1024)S(1)} %reshape.192, ...), kind=kOutput, calls=%fused_computation.41 | convolution fusion | flops 3634885888 | bytes 19288576 | tf_op jit(solution)/shard_map/tn,dnr->tdr/dot_general | solution.py:533
  228.8 1.7 multiply_add_fusion.1
  230.5 1.9 fusion.42
  232.4 1.0 fusion.40
  233.4 1.4 convolution_convert_fusion.do_ref
  234.9 46.3 %shard_map.163 = bf16[1024,2304]{1,0:T(8,128)(2,1)} custom-call(bf16[1024,768]{1,0:T(8,128)(2,1)S(1)} %copy-done.1, bf16[1024,1536]{1,0:T(8,128)(2,1)} %get-tuple-element.26.kv_ref, bf16[64,1536]{1,0:T(8,128)(2,1)S(1)} %get-tuple-element.30.lo_ref, bf16[64,1536]{1,0:T(8,128)(2,1)S(1)} %get-tuple-element.31.hi_ref, s32[1024,1]{1,0:T(8,128)S(1)} %copy.31.tq_ref, ...), custom_call_target="tpu_custom_call" | custom-call | tf_op jit(solution)/shard_map/pallas_call | solution.py:411
  281.2 6.4 %fusion.36 = bf16[2304,384]{1,0:T(8,128)(2,1)} fusion(bf16[1024,2304]{1,0:T(8,128)(2,1)} %shard_map.163, bf16[1024,768]{1,0:T(8,128)(2,1)S(1)} %copy-done.27), kind=kOutput, calls=%fused_computation.74 | convolution fusion | flops 1811939328 | bytes 7274496 | tf_op jit(solution)/shard_map/dot_general | solution.py:540
  287.6 4.2 %fusion.32 = bf16[2304,384]{1,0:T(8,128)(2,1)} fusion(bf16[1024,2304]{1,0:T(8,128)(2,1)S(1)} %copy-done.14, bf16[1024,768]{1,0:T(8,128)(2,1)S(1)} %copy-done.27), kind=kOutput, calls=%fused_computation.70 | convolution fusion | flops 1811939328 | bytes 7274496 | tf_op jit(solution)/shard_map/dot_general | solution.py:540
  291.8 1.2 convolution_bitcast_fusion.3
  293.0 2.4 convolution_bitcast_fusion.2
  295.6 5.9 %fusion.18 = (bf16[768]{0:T(1024)(128)(2,1)S(1)}, f32[1024]{0:T(1024)S(1)}, f32[1024]{0:T(1024)S(1)}, f32[1024,768]{1,0:T(8,128)}) fusion(bf16[1024,768]{1,0:T(8,128)(2,1)S(1)} %copy-done.9, f32[1024]{0:T(1024)S(1)} %add_rsqrt_fusion.1, f32[1024]{0:T(1024)S(1)} %broadcast_multiply_fusion.5, f32[768]{0:T(1024)S(1)} %reshape.191, ...), kind=kOutput, calls=%fused_computation.37 | convolution fusion | flops 3630953728 | bytes 12997120 | tf_op jit(solution)/shard_map/tn,dnr->tdr/dot_general | solution.py:533
  302.3 1.4 reshape_reshape.6
  304.7 1.5 copy.50
  306.2 1.4 reshape_reshape.7
  307.6 0.9 convert_dynamic-update-slice_fusion.6
  308.5 2.9 convert_dynamic-update-slice_fusion.3
  311.4 1.0 convert_dynamic-update-slice_fusion.5
  312.4 1.5 convert_dynamic-update-slice_fusion.2
  314.5 1.4 convert_dynamic-update-slice_fusion.1
  316.0 1.1 convert_dynamic-update-slice_fusion.4
  317.0 1.5 convert_dynamic-update-slice_fusion
  319.2 8.9 %pad_maximum_fusion = bf16[2,6656,384]{2,1,0:T(8,128)(2,1)} fusion(bf16[1,6656,384]{2,1,0:T(8,128)(2,1)} %bitcast.37, bf16[1,6656,384]{2,1,0:T(8,128)(2,1)} %bitcast.99), kind=kLoop, calls=%fused_computation | loop fusion | flops 5111808 | bytes 20447232 | tf_op jit(solution)/shard_map/stack | solution.py:625
  328.1 4.4 %copy.34 = bf16[1024,1152]{0,1:T(8,128)(2,1)} copy(bf16[1024,1152]{1,0:T(8,128)(2,1)} %get-tuple-element.51) | data formatting | bytes 4718592 | tf_op jit(solution)/shard_map/convert_element_type | solution.py:596
  332.6 4.7 %fusion.17 = f32[1024,768]{1,0:T(8,128)} fusion(f32[1024,768]{1,0:T(8,128)S(1)} %copy-done.4, bf16[1024,768]{1,0:T(8,128)(2,1)} %param.10, f32[1024,768]{1,0:T(8,128)} %get-tuple-element.68, f32[1024]{0:T(1024)S(1)} %broadcast_multiply_fusion, f32[1024]{0:T(1024)S(1)} %broadcast_multiply_fusion.1, f32[768]{0:T(1024)S(1)} %reshape.191, ...), kind=kLoop, calls=%fused_computation.36 | loop fusion | flops 7077888 | bytes 11029504 | tf_op jit(solution)/shard_map/add | solution.py:615
  337.6 1.6 copy-done.18
  339.2 1.0 copy-done.20
  340.2 3.5 fusion.20
  343.7 1.8 reduce-scatter.2.cloned.1.call-done
  345.5 2.4 copy-done.2
  347.9 60.1 %shard_map.164 = f32[416,384]{1,0:T(8,128)S(1)} custom-call(bf16[16,416,384]{2,1,0:T(8,128)(2,1)S(1)} %bitcast.89), custom_call_target="tpu_custom_call" | custom-call | tf_op jit(solution)/shard_map/pallas_call | solution.py:210
  (116 shorter events, 15.0 us)
Async XLA Ops:
  7.2 71.4 %all-gather.3.cloned.1.call-start = ((), (), s32[]{:S(2)}) async-start(), calls=%async_computation.1 | async-start | bytes 5068800 | tf_op jit(solution)/shard_map/all_gather | solution.py:514
  9.5 142.3 %all-gather.5.cloned.1.call-start = ((), (), s32[]{:S(2)}) async-start(), calls=%async_computation.2 | async-start | bytes 5677056 | tf_op jit(solution)/shard_map/all_gather | solution.py:514
  15.2 330.2 %reduce-scatter.2.cloned.1.call-start = ((), (), s32[]{:S(2)}) async-start(), calls=%async_computation.3 | async-start | bytes 15335424 | tf_op jit(solution)/shard_map/reduce_scatter | solution.py:647
  16.1 16.4 %collective-permute-start = (s32[64]{0:T(128)S(1)}, s32[64]{0:T(128)S(1)}, u32[]{:S(2)}, u32[]{:S(2)}) collective-permute-start(s32[64]{0:T(128)S(1)} %get-tuple-element.63), channel_id=1, source_target_pairs={{0,1},{1,2},{2,3},{3,4},{4,5},{5,6},{6,7},{7,8},{8,9},{9,10},{10,1... | collective-permute-start | bytes 776 | tf_op jit(solution)/shard_map/ppermute | solution.py:25
  20.9 11.6 %collective-permute-start.1 = (s32[64]{0:T(128)S(1)}, s32[64]{0:T(128)S(1)}, u32[]{:S(2)}, u32[]{:S(2)}) collective-permute-start(s32[64]{0:T(128)S(1)} %get-tuple-element.62), channel_id=1, source_target_pairs={{1,0},{2,1},{3,2},{4,3},{5,4},{6,5},{7,6},{8,7},{9,8},{10,9},{11,1... | collective-permute-start | bytes 776 | tf_op jit(solution)/shard_map/ppermute | solution.py:26
  27.6 3.6 copy-start.7
  84.1 8.2 %copy-start.12 = (bf16[2,16,48,384]{3,2,1,0:T(8,128)(2,1)}, bf16[2,16,48,384]{3,2,1,0:T(8,128)(2,1)S(1)}, u32[]{:S(2)}) copy-start(bf16[2,16,48,384]{3,2,1,0:T(8,128)(2,1)S(1)} %slice.124) | copy-start | bytes 3538948
  92.9 1.2 copy-start.26
  112.1 1.4 copy-start
  113.5 24.8 %copy-start.8 = (bf16[1024,768]{1,0:T(8,128)(2,1)S(1)}, bf16[1024,768]{1,0:T(8,128)(2,1)}, u32[]{:S(2)}) copy-start(bf16[1024,768]{1,0:T(8,128)(2,1)} %param.10) | copy-start | bytes 4718596
  113.5 24.8 %copy-start.13 = (bf16[2,16,48,384]{3,2,1,0:T(8,128)(2,1)S(1)}, bf16[2,16,48,384]{3,2,1,0:T(8,128)(2,1)}, u32[]{:S(2)}) copy-start(bf16[2,16,48,384]{3,2,1,0:T(8,128)(2,1)} %copy-done.12) | copy-start | bytes 3538948
  165.1 1.8 copy-start.24
  166.8 4.7 %copy-start.19 = (bf16[2,16,48,576]{3,2,1,0:T(8,128)(2,1)}, bf16[2,16,48,576]{3,2,1,0:T(8,128)(2,1)S(1)}, u32[]{:S(2)}) copy-start(bf16[2,16,48,576]{3,2,1,0:T(8,128)(2,1)S(1)} %maximum_maximum_fusion) | copy-start | bytes 5308420
  177.6 8.4 %slice-start = ((s8[4718592]{0:T(1024)(128)(4,1)}), s8[4194304]{0:T(1024)(128)(4,1)S(1)}, s32[]{:S(2)}) async-start(s8[4718592]{0:T(1024)(128)(4,1)} %bitcast.91), calls=%async_computation.4 | async-start | bytes 8388608
  180.1 6.0 %slice-start.1 = ((s8[4718592]{0:T(1024)(128)(4,1)}), s8[524288]{0:T(1024)(128)(4,1)S(1)}, s32[]{:S(2)}) async-start(s8[4718592]{0:T(1024)(128)(4,1)} %bitcast.91), calls=%async_computation.5 | async-start | bytes 1048576
  200.9 8.0 %copy-start.11 = (f32[1024,1152]{1,0:T(8,128)}, f32[1024,1152]{1,0:T(8,128)S(1)}, u32[]{:S(2)}) copy-start(f32[1024,1152]{1,0:T(8,128)S(1)} %get-tuple-element.50) | copy-start | bytes 14155780
  200.9 8.0 %copy-start.15 = (f32[1024,1152]{1,0:T(8,128)S(1)}, f32[1024,1152]{1,0:T(8,128)}, u32[]{:S(2)}) copy-start(f32[1024,1152]{1,0:T(8,128)} %get-tuple-element.48) | copy-start | bytes 14155780
  218.5 10.2 %copy-start.5 = (f32[1024,768]{1,0:T(8,128)S(1)}, f32[1024,768]{1,0:T(8,128)}, u32[]{:S(2)}) copy-start(f32[1024,768]{1,0:T(8,128)} %convert_add_fusion) | copy-start | bytes 9437188
  218.5 10.2 %copy-start.25 = (bf16[1024,768]{1,0:T(8,128)(2,1)S(1)}, bf16[1024,768]{1,0:T(8,128)(2,1)}, u32[]{:S(2)}) copy-start(bf16[1024,768]{1,0:T(8,128)(2,1)} %param.19) | copy-start | bytes 4718596
  230.5 2.9 copy-start.3
  230.5 2.9 copy-start.28
  233.4 1.5 copy-start.1
  234.9 46.3 %copy-start.27 = (bf16[1024,768]{1,0:T(8,128)(2,1)S(1)}, bf16[1024,768]{1,0:T(8,128)(2,1)}, u32[]{:S(2)}) copy-start(bf16[1024,768]{1,0:T(8,128)(2,1)} %copy-done.26) | copy-start | bytes 4718596
  281.2 6.4 %copy-start.14 = (bf16[1024,2304]{1,0:T(8,128)(2,1)S(1)}, bf16[1024,2304]{1,0:T(8,128)(2,1)}, u32[]{:S(2)}) copy-start(bf16[1024,2304]{1,0:T(8,128)(2,1)} %shard_map.163) | copy-start | bytes 14155780
  287.6 4.2 %copy-start.10 = (bf16[1024,1152]{1,0:T(8,128)(2,1)S(1)}, bf16[1024,1152]{1,0:T(8,128)(2,1)}, u32[]{:S(2)}) copy-start(bf16[1024,1152]{1,0:T(8,128)(2,1)} %get-tuple-element.51) | copy-start | bytes 7077892
  293.0 2.4 copy-start.9
  293.0 2.6 copy-start.16
  301.4 2.4 copy-start.17
  307.6 4.9 %copy-start.23 = (bf16[2304,384]{1,0:T(8,128)(2,1)S(1)}, bf16[2304,384]{1,0:T(8,128)(2,1)}, u32[]{:S(2)}) copy-start(bf16[2304,384]{1,0:T(8,128)(2,1)} %fusion.36) | copy-start | bytes 5308420
  311.4 3.1 copy-start.21
  313.9 3.1 copy-start.22
  328.1 4.4 %copy-start.4 = (f32[1024,768]{1,0:T(8,128)S(1)}, f32[1024,768]{1,0:T(8,128)}, u32[]{:S(2)}) copy-start(f32[1024,768]{1,0:T(8,128)} %copy-done.3) | copy-start | bytes 9437188
  332.6 5.0 %copy-start.6 = (f32[1024,768]{1,0:T(8,128)S(1)}, f32[1024,768]{1,0:T(8,128)}, u32[]{:S(2)}) copy-start(f32[1024,768]{1,0:T(8,128)} %convert_add_fusion) | copy-start | bytes 9437188
  332.6 6.6 %copy-start.18 = (bf16[1024,1152]{0,1:T(8,128)(2,1)S(1)}, bf16[1024,1152]{0,1:T(8,128)(2,1)}, u32[]{:S(2)}) copy-start(bf16[1024,1152]{0,1:T(8,128)(2,1)} %copy.34) | copy-start | bytes 7077892
  332.6 7.6 %copy-start.20 = (bf16[2,16,48,576]{3,2,1,0:T(8,128)(2,1)S(1)}, bf16[2,16,48,576]{3,2,1,0:T(8,128)(2,1)}, u32[]{:S(2)}) copy-start(bf16[2,16,48,576]{3,2,1,0:T(8,128)(2,1)} %copy-done.19) | copy-start | bytes 5308420
  345.5 2.4 copy-start.2
Sparse Core Ops, SparseCore 0:
  11.4 67.0 all-gather.2
  82.0 69.7 all-gather.4
  328.3 17.1 reduce-scatter.1
